TPU v7x, 32 devices: a whole 2x2x4 slice. The times are simulated.
32 devices in a mesh: shard: 8 (over y, x, core), replica: 4 (over z).
Axes of the slice: x: 2, y: 2, z: 4, core: 2. Of those that a mesh axis runs over, the one named last changes fastest.
Arguments:
- hidden: bfloat16 [8192, 768], P(('replica', 'shard')), may hold values from -6 to 6
- segment_ids: int32 [8192], P(('replica', 'shard')), may hold values from 0 to 63, as said below
- w_qkv: bfloat16 [768, 2304], P('shard'), may hold values from -0.21875 to 0.21875
- b_qv: bfloat16 [2, 768], P(None, 'shard'), may hold values from -3 to 3
- w_out: bfloat16 [768, 768], P('shard'), may hold values from -3 to 3
- b_out: bfloat16 [768], P('shard'), may hold values from -3 to 3
- gain1: bfloat16 [768], P('shard'), may hold values from 0.5 to 1.5
- shift1: bfloat16 [768], P('shard'), may hold values from -3 to 3
- w_in: bfloat16 [768, 3072], P('shard'), may hold values from -0.21875 to 0.21875
- b_in: bfloat16 [3072], P('shard'), may hold values from -3 to 3
- w_back: bfloat16 [3072, 768], P('shard'), may hold values from -0.21875 to 0.21875
- b_back: bfloat16 [768], P('shard'), may hold values from -3 to 3
- gain2: bfloat16 [768], P('shard'), may hold values from 0.5 to 1.5
- shift2: bfloat16 [768], P('shard'), may hold values from -3 to 3
- cotangent: float32 [8192, 768], P(('replica', 'shard')), may hold values from -6 to 6
Outputs:
- output: bfloat16 [8192, 768], P(('replica', 'shard'))
- d_hidden: float32 [8192, 768], P(('replica', 'shard'))
- grad_w_qkv: float32 [768, 2304], P('shard')
- grad_b_qv: float32 [2, 768], P(None, 'shard')
- grad_w_out: float32 [768, 768], P('shard')
- grad_b_out: float32 [768], P('shard')
- grad_gain1: float32 [768], P('shard')
- grad_shift1: float32 [768], P('shard')
- grad_w_in: float32 [768, 3072], P('shard')
- grad_b_in: float32 [3072], P('shard')
- grad_w_back: float32 [3072, 768], P('shard')
- grad_b_back: float32 [768], P('shard')
- grad_gain2: float32 [768], P('shard')
- grad_shift2: float32 [768], P('shard')
Inputs may be any that keep to these rules, and one draw needn't show every extreme that they name: `segment_ids`: ids never fall along the tokens. Sequence s (tokens s * 2048 to (s + 1) * 2048 - 1) holds exactly 16 documents with ids s * 16 to s * 16 + 15, one of them 1280 tokens long.
All inputs are finite; a program needn't handle non-finite values.
Results may differ from a plain program's by a relative error of at most 0.023.
Values may be sent and summed in bfloat16 or wider, within the bound.
A program may use at most 192 MiB of HBM per device.

v0:
```python
import math
import jax
import jax.numpy as jnp
from jax import lax
from jax.sharding import PartitionSpec as P

HEADS = 12
scale_factor = 0.125
norm_epsilon = 1e-05
masked_value = -1e30


def normalize(resid, gain, shift):
    mean_value = jnp.mean(resid, axis=-1, keepdims=True)
    centered = resid - mean_value
    variance = jnp.mean(centered * centered, axis=-1, keepdims=True)
    return centered * lax.rsqrt(variance + norm_epsilon) * gain + shift


def gelu_exact(values):
    return jax.nn.gelu(values, approximate=False)


def keep_state(state):
    return state


def block_size(count):
    return math.gcd(count, 512)


def masked_scores(query_heads, key_heads, query_segs, key_segs):
    scores = (
        jnp.einsum("qhd,khd->hqk", query_heads, key_heads, preferred_element_type=jnp.float32)
        * scale_factor
    )
    allowed = query_segs[:, None] == key_segs[None, :]
    return (scores, allowed[None])


def grad_block(
    query_heads, dctx_heads, log_total, delta, query_segs, key_heads, value_heads, key_segs
):
    scores, allowed = masked_scores(query_heads, key_heads, query_segs, key_segs)
    probs = jnp.where(allowed, jnp.exp(scores - log_total[:, :, None]), 0.0)
    d_prob = jnp.einsum("qhd,khd->hqk", dctx_heads, value_heads, preferred_element_type=jnp.float32)
    d_scores = (probs * (d_prob - delta[:, :, None])).astype(jnp.bfloat16)
    return (probs.astype(jnp.bfloat16), d_scores)


def body(
    hidden,
    segment_ids,
    w_qkv,
    b_qv,
    w_out,
    b_out,
    gain1,
    shift1,
    w_in,
    b_in,
    w_back,
    b_back,
    gain2,
    shift2,
    cotangent,
):
    tok_rows, width = hidden.shape
    heads = HEADS
    head_dim = width // heads
    seg_low = segment_ids[0]
    seg_high = segment_ids[-1]
    wq_full, wo_full, bqv_full, bo_full, g1_full, s1_full = (
        lax.all_gather(w_qkv, "shard", axis=0, tiled=True),
        lax.all_gather(w_out, "shard", axis=0, tiled=True),
        lax.all_gather(b_qv, "shard", axis=1, tiled=True),
        lax.all_gather(b_out, "shard", axis=0, tiled=True),
        lax.all_gather(gain1, "shard", axis=0, tiled=True),
        lax.all_gather(shift1, "shard", axis=0, tiled=True),
    )
    qkv = jnp.dot(hidden, wq_full, preferred_element_type=jnp.float32)
    bqv_wide = bqv_full.astype(jnp.float32)
    query = (qkv[:, :width] + bqv_wide[0]).astype(jnp.bfloat16)
    keys = qkv[:, width : 2 * width].astype(jnp.bfloat16)
    values = (qkv[:, 2 * width :] + bqv_wide[1]).astype(jnp.bfloat16)
    query_heads = query.reshape(tok_rows, heads, head_dim)
    key_local = keys.reshape(tok_rows, heads, head_dim)
    value_local = values.reshape(tok_rows, heads, head_dim)
    start_state = (
        jnp.full((heads, tok_rows), masked_value, jnp.float32),
        jnp.zeros((heads, tok_rows), jnp.float32),
        jnp.zeros((tok_rows, heads, head_dim), jnp.float32),
    )
    key_piece = lax.all_gather(keys, "shard", axis=0, tiled=True)
    value_piece = lax.all_gather(values, "shard", axis=0, tiled=True)
    seg_piece = lax.all_gather(segment_ids, "shard", axis=0, tiled=True)
    count = key_piece.shape[0]
    block = block_size(count)

    def forward_step(index, state):
        offset = index * block
        key_heads = lax.dynamic_slice_in_dim(key_piece, offset, block, 0).reshape(
            block, heads, head_dim
        )
        value_heads = lax.dynamic_slice_in_dim(value_piece, offset, block, 0).reshape(
            block, heads, head_dim
        )
        key_segs = lax.dynamic_slice_in_dim(seg_piece, offset, block, 0)

        def forward_update(state):
            running_max, running_sum, accum = state
            scores, allowed = masked_scores(query_heads, key_heads, segment_ids, key_segs)
            new_max = jnp.maximum(
                running_max, jnp.max(jnp.where(allowed, scores, masked_value), axis=-1)
            )
            factor = jnp.exp(running_max - new_max)
            weights = jnp.where(allowed, jnp.exp(scores - new_max[:, :, None]), 0.0)
            running_sum = running_sum * factor + jnp.sum(weights, axis=-1)
            accum = accum * factor.T[:, :, None] + jnp.einsum(
                "hqk,khd->qhd",
                weights.astype(jnp.bfloat16),
                value_heads,
                preferred_element_type=jnp.float32,
            )
            return (new_max, running_sum, accum)

        touches = jnp.logical_and(key_segs[0] <= seg_high, key_segs[-1] >= seg_low)
        return lax.cond(touches, forward_update, keep_state, state)

    running_max, running_sum, accum = lax.fori_loop(0, count // block, forward_step, start_state)
    context32 = accum / running_sum.T[:, :, None]
    log_total = running_max + jnp.log(running_sum)
    context = context32.reshape(tok_rows, width).astype(jnp.bfloat16)
    resid1 = (
        hidden.astype(jnp.float32)
        + jnp.dot(context, wo_full, preferred_element_type=jnp.float32)
        + bo_full.astype(jnp.float32)
    )
    normed1, norm1_pull = jax.vjp(
        normalize, resid1, g1_full.astype(jnp.float32), s1_full.astype(jnp.float32)
    )
    wi_full, bi_full, wb_full, bb_full, g2_full, s2_full = (
        lax.all_gather(w_in, "shard", axis=0, tiled=True),
        lax.all_gather(b_in, "shard", axis=0, tiled=True),
        lax.all_gather(w_back, "shard", axis=0, tiled=True),
        lax.all_gather(b_back, "shard", axis=0, tiled=True),
        lax.all_gather(gain2, "shard", axis=0, tiled=True),
        lax.all_gather(shift2, "shard", axis=0, tiled=True),
    )
    normed1_low = normed1.astype(jnp.bfloat16)
    pre = jnp.dot(normed1_low, wi_full, preferred_element_type=jnp.float32) + bi_full.astype(
        jnp.float32
    )
    act, gelu_pull = jax.vjp(gelu_exact, pre)
    act_low = act.astype(jnp.bfloat16)
    resid2 = (
        normed1
        + jnp.dot(act_low, wb_full, preferred_element_type=jnp.float32)
        + bb_full.astype(jnp.float32)
    )
    out32, norm2_pull = jax.vjp(
        normalize, resid2, g2_full.astype(jnp.float32), s2_full.astype(jnp.float32)
    )
    output = out32.astype(jnp.bfloat16)
    d_resid2, grad_gain2, grad_shift2 = norm2_pull(cotangent)
    d_branch2 = d_resid2.astype(jnp.bfloat16)
    grad_b_back = jnp.sum(d_resid2, axis=0)
    grad_w_back = jnp.einsum("tf,td->fd", act_low, d_branch2, preferred_element_type=jnp.float32)
    d_act = jnp.einsum("td,fd->tf", d_branch2, wb_full, preferred_element_type=jnp.float32)
    (d_pre,) = gelu_pull(d_act)
    grad_b_in = jnp.sum(d_pre, axis=0)
    d_pre_low = d_pre.astype(jnp.bfloat16)
    grad_w_in = jnp.einsum("td,tf->df", normed1_low, d_pre_low, preferred_element_type=jnp.float32)
    d_normed1 = d_resid2 + jnp.einsum(
        "tf,df->td", d_pre_low, wi_full, preferred_element_type=jnp.float32
    )
    d_resid1, grad_gain1, grad_shift1 = norm1_pull(d_normed1)
    grad_b_out = jnp.sum(d_resid1, axis=0)
    d_branch1 = d_resid1.astype(jnp.bfloat16)
    grad_w_out = jnp.einsum("tc,td->cd", context, d_branch1, preferred_element_type=jnp.float32)
    d_context = jnp.einsum(
        "td,cd->tc", d_branch1, wo_full, preferred_element_type=jnp.float32
    ).astype(jnp.bfloat16)
    dctx_heads = d_context.reshape(tok_rows, heads, head_dim)
    delta = jnp.einsum("qhd,qhd->hq", dctx_heads.astype(jnp.float32), context32)
    zero_heads = jnp.zeros((tok_rows, heads, head_dim), jnp.float32)
    query_key_piece = lax.all_gather(keys, "shard", axis=0, tiled=True)
    query_value_piece = lax.all_gather(values, "shard", axis=0, tiled=True)
    query_seg_piece = lax.all_gather(segment_ids, "shard", axis=0, tiled=True)
    count = query_key_piece.shape[0]
    query_block = block_size(count)

    def query_step(index, summed):
        offset = index * query_block
        key_heads = lax.dynamic_slice_in_dim(query_key_piece, offset, query_block, 0).reshape(
            query_block, heads, head_dim
        )
        value_heads = lax.dynamic_slice_in_dim(query_value_piece, offset, query_block, 0).reshape(
            query_block, heads, head_dim
        )
        key_segs = lax.dynamic_slice_in_dim(query_seg_piece, offset, query_block, 0)

        def query_update(summed):
            probs, d_scores = grad_block(
                query_heads,
                dctx_heads,
                log_total,
                delta,
                segment_ids,
                key_heads,
                value_heads,
                key_segs,
            )
            return (
                summed
                + jnp.einsum(
                    "hqk,khd->qhd", d_scores, key_heads, preferred_element_type=jnp.float32
                )
                * scale_factor
            )

        touches = jnp.logical_and(key_segs[0] <= seg_high, key_segs[-1] >= seg_low)
        return lax.cond(touches, query_update, keep_state, summed)

    d_query = lax.fori_loop(0, count // query_block, query_step, zero_heads)
    all_log_total, all_delta = (
        lax.all_gather(log_total, "shard", axis=1, tiled=True),
        lax.all_gather(delta, "shard", axis=1, tiled=True),
    )
    query_piece = lax.all_gather(query, "shard", axis=0, tiled=True)
    dctx_piece = lax.all_gather(d_context, "shard", axis=0, tiled=True)
    key_seg_piece = lax.all_gather(segment_ids, "shard", axis=0, tiled=True)
    count = query_piece.shape[0]
    key_block = block_size(count)

    def key_step(index, state):
        offset = index * key_block
        piece_query = lax.dynamic_slice_in_dim(query_piece, offset, key_block, 0).reshape(
            key_block, heads, head_dim
        )
        piece_dctx = lax.dynamic_slice_in_dim(dctx_piece, offset, key_block, 0).reshape(
            key_block, heads, head_dim
        )
        piece_segs = lax.dynamic_slice_in_dim(key_seg_piece, offset, key_block, 0)
        piece_log = lax.dynamic_slice_in_dim(all_log_total, offset, key_block, 1)
        piece_delta = lax.dynamic_slice_in_dim(all_delta, offset, key_block, 1)

        def key_update(state):
            d_key, d_value = state
            probs, d_scores = grad_block(
                piece_query,
                piece_dctx,
                piece_log,
                piece_delta,
                piece_segs,
                key_local,
                value_local,
                segment_ids,
            )
            d_key = (
                d_key
                + jnp.einsum(
                    "hqk,qhd->khd", d_scores, piece_query, preferred_element_type=jnp.float32
                )
                * scale_factor
            )
            d_value = d_value + jnp.einsum(
                "hqk,qhd->khd", probs, piece_dctx, preferred_element_type=jnp.float32
            )
            return (d_key, d_value)

        touches = jnp.logical_and(piece_segs[0] <= seg_high, piece_segs[-1] >= seg_low)
        return lax.cond(touches, key_update, keep_state, state)

    d_key_heads, d_value_heads = lax.fori_loop(
        0, count // key_block, key_step, (zero_heads, zero_heads)
    )
    d_keys = d_key_heads.reshape(tok_rows, width)
    d_values = d_value_heads.reshape(tok_rows, width)
    d_query = d_query.reshape(tok_rows, width)
    grad_b_qv = jnp.stack([jnp.sum(d_query, axis=0), jnp.sum(d_values, axis=0)], axis=0)
    d_qkv = jnp.concatenate([d_query, d_keys, d_values], axis=1).astype(jnp.bfloat16)
    grad_w_qkv = jnp.einsum("td,te->de", hidden, d_qkv, preferred_element_type=jnp.float32)
    d_hidden = d_resid1 + jnp.einsum(
        "te,de->td", d_qkv, wq_full, preferred_element_type=jnp.float32
    )
    local_grads = (
        grad_w_qkv,
        grad_b_qv,
        grad_w_out,
        grad_b_out,
        grad_gain1,
        grad_shift1,
        grad_w_in,
        grad_b_in,
        grad_w_back,
        grad_b_back,
        grad_gain2,
        grad_shift2,
    )
    shard_grads = (
        lax.psum_scatter(
            local_grads[0].astype(jnp.bfloat16), "shard", scatter_dimension=0, tiled=True
        ).astype(jnp.float32),
        lax.psum_scatter(
            local_grads[1].astype(jnp.bfloat16), "shard", scatter_dimension=1, tiled=True
        ).astype(jnp.float32),
        lax.psum_scatter(
            local_grads[2].astype(jnp.bfloat16), "shard", scatter_dimension=0, tiled=True
        ).astype(jnp.float32),
        lax.psum_scatter(
            local_grads[3].astype(jnp.bfloat16), "shard", scatter_dimension=0, tiled=True
        ).astype(jnp.float32),
        lax.psum_scatter(
            local_grads[4].astype(jnp.bfloat16), "shard", scatter_dimension=0, tiled=True
        ).astype(jnp.float32),
        lax.psum_scatter(
            local_grads[5].astype(jnp.bfloat16), "shard", scatter_dimension=0, tiled=True
        ).astype(jnp.float32),
        lax.psum_scatter(
            local_grads[6].astype(jnp.bfloat16), "shard", scatter_dimension=0, tiled=True
        ).astype(jnp.float32),
        lax.psum_scatter(
            local_grads[7].astype(jnp.bfloat16), "shard", scatter_dimension=0, tiled=True
        ).astype(jnp.float32),
        lax.psum_scatter(
            local_grads[8].astype(jnp.bfloat16), "shard", scatter_dimension=0, tiled=True
        ).astype(jnp.float32),
        lax.psum_scatter(
            local_grads[9].astype(jnp.bfloat16), "shard", scatter_dimension=0, tiled=True
        ).astype(jnp.float32),
        lax.psum_scatter(
            local_grads[10].astype(jnp.bfloat16), "shard", scatter_dimension=0, tiled=True
        ).astype(jnp.float32),
        lax.psum_scatter(
            local_grads[11].astype(jnp.bfloat16), "shard", scatter_dimension=0, tiled=True
        ).astype(jnp.float32),
    )
    total_grads = (
        lax.psum(shard_grads[0].astype(jnp.bfloat16), "replica").astype(jnp.float32),
        lax.psum(shard_grads[1].astype(jnp.bfloat16), "replica").astype(jnp.float32),
        lax.psum(shard_grads[2].astype(jnp.bfloat16), "replica").astype(jnp.float32),
        lax.psum(shard_grads[3].astype(jnp.bfloat16), "replica").astype(jnp.float32),
        lax.psum(shard_grads[4].astype(jnp.bfloat16), "replica").astype(jnp.float32),
        lax.psum(shard_grads[5].astype(jnp.bfloat16), "replica").astype(jnp.float32),
        lax.psum(shard_grads[6].astype(jnp.bfloat16), "replica").astype(jnp.float32),
        lax.psum(shard_grads[7].astype(jnp.bfloat16), "replica").astype(jnp.float32),
        lax.psum(shard_grads[8].astype(jnp.bfloat16), "replica").astype(jnp.float32),
        lax.psum(shard_grads[9].astype(jnp.bfloat16), "replica").astype(jnp.float32),
        lax.psum(shard_grads[10].astype(jnp.bfloat16), "replica").astype(jnp.float32),
        lax.psum(shard_grads[11].astype(jnp.bfloat16), "replica").astype(jnp.float32),
    )
    return (output, d_hidden) + tuple(total_grads)


def solution(mesh):
    in_specs = (
        P(("replica", "shard"), None),
        P(("replica", "shard")),
        P("shard", None),
        P(None, "shard"),
        P("shard", None),
        P("shard"),
        P("shard"),
        P("shard"),
        P("shard", None),
        P("shard"),
        P("shard", None),
        P("shard"),
        P("shard"),
        P("shard"),
        P(("replica", "shard"), None),
    )
    out_specs = (
        P(("replica", "shard"), None),
        P(("replica", "shard"), None),
        P("shard", None),
        P(None, "shard"),
        P("shard", None),
        P("shard"),
        P("shard"),
        P("shard"),
        P("shard", None),
        P("shard"),
        P("shard", None),
        P("shard"),
        P("shard"),
        P("shard"),
    )
    return jax.shard_map(body, mesh=mesh, in_specs=in_specs, out_specs=out_specs, check_vma=False)
```

profile of v0, /device:TPU:0, one launch (start us, length us, event | category | flops | bytes accessed | tf_op | source)
XLA Modules:
  0.0 788.4 jit_solution(2066285224074038387)
XLA Ops:
  8.0 38.5 %all-gather.12.cloned.1.call-done = bf16[768,2304]{1,0:T(8,128)(2,1)} async-done(((bf16[96,2304]{1,0:T(8,128)(2,1)}), bf16[768,2304]{1,0:T(8,128)(2,1)}) %all-gather.12.cloned.1.call-update) | async-done | bytes 3538960 | tf_op jit(solution)/shard_map/all_gather | solution.py:74
  64.7 24.2 %all-reduce.14 = (bf16[768]{0:T(1024)(128)(2,1)S(1)}, bf16[768]{0:T(1024)(128)(2,1)S(1)}, bf16[768]{0:T(1024)(128)(2,1)S(1)}, bf16[768]{0:T(1024)(128)(2,1)S(1)}, bf16[768]{0:T(1024)(128)(2,1)S(1)}) all-reduce(bf16[768]{0:T(1024)(128)(2,1)S(1)} %dynamic-update-slice, ...), channel_id=1, replica_groups=mesh['shard'=8,'replica'=4] {'shard'}, use_global_device_ids=true, to_apply=%add | all-reduce | flops 3840 | bytes 15360
  97.0 8.8 %all-gather = s32[8,1,256]{2,1,0:T(1,128)} all-gather(s32[1,1,256]{2,1,0:T(1,128)S(1)} %bitcast.168), channel_id=1, replica_groups=mesh['shard'=8,'replica'=4] {'shard'}, dimensions={0}, use_global_device_ids=true | all-gather | bytes 9216 | tf_op jit(solution)/shard_map/all_gather | solution.py:96
  122.7 32.9 %while.48 = (s32[]{:T(128)}, f32[12,256]{1,0:T(8,128)S(1)}, f32[12,256]{1,0:T(8,128)S(1)}, f32[256,12,64]{0,2,1:T(8,128)S(1)}, s32[2048]{0:T(1024)}, /*index=5*/...) while((s32[]{:T(128)}, f32[12,256]{1,0:T(8,128)S(1)}, ...), condition=%wide.region_5.6_spmd, body=%wide.region_0.5_spmd.sunk | while | flops 420488192 | bytes 26287476 | solution.py:130
  158.3 25.8 %all-gather.20.cloned.1.call-done = bf16[768,3072]{1,0:T(8,128)(2,1)} async-done(((bf16[96,3072]{1,0:T(8,128)(2,1)}), bf16[768,3072]{1,0:T(8,128)(2,1)}) %all-gather.20.cloned.1.call-update) | async-done | bytes 4718608 | tf_op jit(solution)/shard_map/all_gather | solution.py:143
  184.0 12.1 %multiply_convert_fusion.8 = (bf16[256,3072]{1,0:T(8,128)(2,1)}, f32[256,3072]{1,0:T(8,128)}, f32[256,3072]{1,0:T(8,128)}) fusion(f32[3072]{0:T(1024)S(1)} %bitcast.171, bf16[768,3072]{1,0:T(8,128)(2,1)} %all-gather.20.cloned.1.call-done, f32[256,768]{1,0:T(8,128)S(1)} %get-tuple-element.1246, f32[768]{0:T(1024)S(1)} %convert_element_type.209, ...), kind=kOutput, calls=%fused_computation.63 | convolution fusion | flops 1260847104 | bytes 13389824 | tf_op jit(solution)/shard_map/dot_general | solution.py:151
  196.1 28.4 %all-gather.22.cloned.1.call-done = bf16[3072,768]{1,0:T(8,128)(2,1)} async-done(((bf16[384,768]{1,0:T(8,128)(2,1)}), bf16[3072,768]{1,0:T(8,128)(2,1)}) %all-gather.22.cloned.1.call-update) | async-done | bytes 4718608 | tf_op jit(solution)/shard_map/all_gather | solution.py:145
  242.4 16.2 %all-gather.24.cloned.1.call-done = bf16[2048,768]{1,0:T(8,128)(2,1)} async-done(((bf16[256,768]{1,0:T(8,128)(2,1)}), bf16[2048,768]{1,0:T(8,128)(2,1)}) %all-gather.24.cloned.1.call-update) | async-done | bytes 3145744 | tf_op jit(solution)/shard_map/all_gather | solution.py:230
  264.1 9.3 %all_gather.77 = f32[12,2048]{1,0:T(8,128)S(1)} all-gather(f32[12,256]{1,0:T(8,128)} %log_add_fusion), channel_id=1, replica_groups=mesh['shard'=8,'replica'=4] {'shard'}, dimensions={1}, use_global_device_ids=true | all-gather | bytes 110592 | tf_op jit(solution)/shard_map/all_gather | solution.py:227
  284.6 51.7 %while.49 = (s32[]{:T(128)}, f32[256,12,64]{0,2,1:T(8,128)}, s32[2048]{0:T(1024)}, s32[]{:T(128)}, s32[]{:T(128)}, /*index=5*/s32[256]{0:T(256)}, bf16[2048,768]...) while((s32[]{:T(128)}, f32[256,12,64]{0,2,1:T(8,128)}, ...), condition=%wide.region_17.18_spmd, body=%wide.region_14.17_spmd.sunk | while | flops 613941248 | bytes 20745584 | solution.py:225
  288.8 11.8 %conditional.7 = (f32[256,12,64]{0,2,1:T(8,128)}) conditional(s32[]{:T(128)} %convert_element_type.315, f32[256,12,64]{0,2,1:T(8,128)} %get-tuple-element.1570, (s32[256]{0:T(256)}, s32[512]{0:T(512)S(1)}, bf16[2048,768]{0,1:T(8,128)(2,1)}, s32[]{:T(128)}, bf16[256,12,64]{0,2,1:T(8,128)(2,1)S(1)}, /*index=5*/f32[12,256]{1,0:T(8,128)}, ...), branch_computations={%region_15.15_spmd, %region_16.16_spmd} | conditional | flops 613941248 | bytes 20741160 | solution.py:223
  304.7 11.8 %conditional.7 = (f32[256,12,64]{0,2,1:T(8,128)}) conditional(s32[]{:T(128)} %convert_element_type.315, f32[256,12,64]{0,2,1:T(8,128)} %get-tuple-element.1570, (s32[256]{0:T(256)}, s32[512]{0:T(512)S(1)}, bf16[2048,768]{0,1:T(8,128)(2,1)}, s32[]{:T(128)}, bf16[256,12,64]{0,2,1:T(8,128)(2,1)S(1)}, /*index=5*/f32[12,256]{1,0:T(8,128)}, ...), branch_computations={%region_15.15_spmd, %region_16.16_spmd} | conditional | flops 613941248 | bytes 20741160 | solution.py:223
  320.5 11.8 %conditional.7 = (f32[256,12,64]{0,2,1:T(8,128)}) conditional(s32[]{:T(128)} %convert_element_type.315, f32[256,12,64]{0,2,1:T(8,128)} %get-tuple-element.1570, (s32[256]{0:T(256)}, s32[512]{0:T(512)S(1)}, bf16[2048,768]{0,1:T(8,128)(2,1)}, s32[]{:T(128)}, bf16[256,12,64]{0,2,1:T(8,128)(2,1)S(1)}, /*index=5*/f32[12,256]{1,0:T(8,128)}, ...), branch_computations={%region_15.15_spmd, %region_16.16_spmd} | conditional | flops 613941248 | bytes 20741160 | solution.py:223
  342.9 66.5 %while.50 = (s32[]{:T(128)}, f32[256,12,64]{0,2,1:T(8,128)}, f32[256,12,64]{0,2,1:T(8,128)}, s32[2048]{0:T(1024)}, s32[]{:T(128)}, /*index=5*/s32[]{:T(128)}, s3...) while((s32[]{:T(128)}, f32[256,12,64]{0,2,1:T(8,128)}, ...), condition=%wide.region_21.22_spmd, body=%wide.region_18.21_spmd.sunk | while | flops 821755904 | bytes 29670792 | solution.py:275
  346.9 16.9 %conditional.8 = ((f32[256,12,64]{0,2,1:T(8,128)}, f32[256,12,64]{0,2,1:T(8,128)})) conditional(s32[]{:T(128)} %convert_element_type.316, (f32[256,12,64]{0,2,1:T(8,128)}, f32[256,12,64]{0,2,1:T(8,128)}) %tuple.174, (s32[512]{0:T(512)S(1)}, s32[256]{0:T(256)S(1)}, bf16[2048,768]{0,1:T(8,128)(2,1)}, s32[]{:T(128)}, ...), branch_computations={%region_19.19_spmd, %region_20.20_spmd} | conditional | flops 821755904 | bytes 29666336 | solution.py:273
  367.7 16.9 %conditional.8 = ((f32[256,12,64]{0,2,1:T(8,128)}, f32[256,12,64]{0,2,1:T(8,128)})) conditional(s32[]{:T(128)} %convert_element_type.316, (f32[256,12,64]{0,2,1:T(8,128)}, f32[256,12,64]{0,2,1:T(8,128)}) %tuple.174, (s32[512]{0:T(512)S(1)}, s32[256]{0:T(256)S(1)}, bf16[2048,768]{0,1:T(8,128)(2,1)}, s32[]{:T(128)}, ...), branch_computations={%region_19.19_spmd, %region_20.20_spmd} | conditional | flops 821755904 | bytes 29666336 | solution.py:273
  388.6 16.9 %conditional.8 = ((f32[256,12,64]{0,2,1:T(8,128)}, f32[256,12,64]{0,2,1:T(8,128)})) conditional(s32[]{:T(128)} %convert_element_type.316, (f32[256,12,64]{0,2,1:T(8,128)}, f32[256,12,64]{0,2,1:T(8,128)}) %tuple.174, (s32[512]{0:T(512)S(1)}, s32[256]{0:T(256)S(1)}, bf16[2048,768]{0,1:T(8,128)(2,1)}, s32[]{:T(128)}, ...), branch_computations={%region_19.19_spmd, %region_20.20_spmd} | conditional | flops 821755904 | bytes 29666336 | solution.py:273
  440.5 58.1 %reduce-scatter.16.cloned.1.call-done = bf16[96,2304]{1,0:T(8,128)(2,1)} async-done(((bf16[768,2304]{1,0:T(8,128)(2,1)}), bf16[96,2304]{1,0:T(8,128)(2,1)}) %reduce-scatter.16.cloned.1.call-update) | async-done | bytes 442384
  500.8 38.3 %reduce-scatter.10.cloned.1.call-done = bf16[96,768]{1,0:T(8,128)(2,1)} async-done(((bf16[768,768]{1,0:T(8,128)(2,1)}), bf16[96,768]{1,0:T(8,128)(2,1)}) %reduce-scatter.10.cloned.1.call-update) | async-done | bytes 147472 | tf_op jit(solution)/shard_map/reduce_scatter | solution.py:308
  539.1 57.3 %reduce-scatter.12.cloned.1.call-done = bf16[96,3072]{1,0:T(8,128)(2,1)} async-done(((bf16[768,3072]{1,0:T(8,128)(2,1)}), bf16[96,3072]{1,0:T(8,128)(2,1)}) %reduce-scatter.12.cloned.1.call-update) | async-done | bytes 589840 | tf_op jit(solution)/shard_map/reduce_scatter | solution.py:320
  596.3 57.1 %reduce-scatter.14.cloned.1.call-done = bf16[384,768]{1,0:T(8,128)(2,1)} async-done(((bf16[3072,768]{1,0:T(8,128)(2,1)}), bf16[384,768]{1,0:T(8,128)(2,1)}) %reduce-scatter.14.cloned.1.call-update) | async-done | bytes 589840 | tf_op jit(solution)/shard_map/reduce_scatter | solution.py:326
  658.2 23.6 %all-reduce.13 = (bf16[768]{0:T(1024)(128)(2,1)S(1)}, bf16[768]{0:T(1024)(128)(2,1)S(1)}, bf16[768]{0:T(1024)(128)(2,1)S(1)}, bf16[768]{0:T(1024)(128)(2,1)S(1)}...) all-reduce(bf16[768]{0:T(1024)(128)(2,1)} %dynamic-update-slice.5, ...), channel_id=1, replica_groups=mesh['shard'=8,'replica'=4] {'shard'}, use_global_device_ids=true, to_apply=%add.5 | all-reduce | flops 8448 | bytes 33792
  691.5 11.9 %all-reduce.15 = (bf16[2,96]{1,0:T(2,128)(2,1)S(1)}, bf16[96]{0:T(256)(128)(2,1)S(1)}, bf16[96]{0:T(256)(128)(2,1)S(1)}, bf16[96]{0:T(256)(128)(2,1)S(1)}, bf16[...) all-reduce(bf16[2,96]{1,0:T(2,128)(2,1)S(1)} %copy.95, ...), channel_id=1, replica_groups=mesh['shard'=8,'replica'=4] {'replica'}, use_global_device_ids=true, to_apply=%region_27.28 | all-reduce | flops 1152 | bytes 4608 | tf_op jit(solution)/shard_map/psum | solution.py:341
  707.7 66.8 %all-reduce.19.cloned.1.call-done = (bf16[96,2304]{0,1:T(8,128)(2,1)}, bf16[96,768]{1,0:T(8,128)(2,1)}, bf16[96,3072]{1,0:T(8,128)(2,1)}, bf16[384,768]{1,0:T(8,128)(2,1)}) async-done(((bf16[96,2304]{0,1:T(8,128)(2,1)}, bf16[96,768]{1,0:T(8,128)(2,1)}, bf16[96,3072]{1,0:T(8,128)(2,1)}, bf16[384,768]{1,0:T(8,128)(2,1)}), (bf16[96,2304]{0,1:T(8,128)(2,1)}, bf16[96,768]{1,0:T(8,128)(2,1)}, ...) | async-done | bytes 1769488 | tf_op jit(solution)/shard_map/psum | solution.py:340
  (333 shorter events, 280.0 us)
Async XLA Ops:
  7.2 39.3 %all-gather.12.cloned.1.call-start = ((), (), s32[]{:S(2)}) async-start(), calls=%async_computation.5 | async-start | bytes 3981312 | tf_op jit(solution)/shard_map/all_gather | solution.py:74
  7.9 99.1 %all-gather.14.cloned.1.call-start = ((), (), s32[]{:S(2)}) async-start(), calls=%async_computation.6 | async-start | bytes 3538944 | tf_op jit(solution)/shard_map/all_gather | solution.py:94
  49.8 47.2 %copy-start.20 = (s32[256]{0:T(256)S(1)}, s32[256]{0:T(256)}, u32[]{:S(2)}) copy-start(s32[256]{0:T(256)} %param.28) | copy-start | bytes 3076
  50.6 67.2 %all-gather.16.cloned.1.call-start = ((), (), s32[]{:S(2)}) async-start(), calls=%async_computation.7 | async-start | bytes 3538944 | tf_op jit(solution)/shard_map/all_gather | solution.py:95
  60.4 95.2 %all-gather.18.cloned.1.call-start = ((), (), s32[]{:S(2)}) async-start(), calls=%async_computation.8 | async-start | bytes 1327104 | tf_op jit(solution)/shard_map/all_gather | solution.py:75
  61.0 123.0 %all-gather.20.cloned.1.call-start = ((), (), s32[]{:S(2)}) async-start(), calls=%async_computation.9 | async-start | bytes 5308416 | tf_op jit(solution)/shard_map/all_gather | solution.py:143
  61.6 163.0 %all-gather.22.cloned.1.call-start = ((), (), s32[]{:S(2)}) async-start(), calls=%async_computation.10 | async-start | bytes 5308416 | tf_op jit(solution)/shard_map/all_gather | solution.py:145
  62.2 196.5 %all-gather.24.cloned.1.call-start = ((), (), s32[]{:S(2)}) async-start(), calls=%async_computation.11 | async-start | bytes 3538944 | tf_op jit(solution)/shard_map/all_gather | solution.py:230
  97.0 127.6 %copy-start.25 = (f32[768]{0:T(1024)}, f32[768]{0:T(1024)S(1)}, u32[]{:S(2)}) copy-start(f32[768]{0:T(1024)S(1)} %convert_element_type.209) | copy-start | bytes 9220
  97.0 139.6 %copy-start.23 = (f32[768]{0:T(1024)}, f32[768]{0:T(1024)S(1)}, u32[]{:S(2)}) copy-start(f32[768]{0:T(1024)S(1)} %convert_element_type.208) | copy-start | bytes 9220
  97.0 133.3 %copy-start.27 = (f32[768]{0:T(1024)}, f32[768]{0:T(1024)S(1)}, u32[]{:S(2)}) copy-start(f32[768]{0:T(1024)S(1)} %convert_element_type.214) | copy-start | bytes 9220
  106.7 229.7 %all-gather.26.cloned.1.call-start = ((), (), s32[]{:S(2)}) async-start(), calls=%async_computation.12 | async-start | bytes 3538944 | tf_op jit(solution)/shard_map/all_gather | solution.py:231
  158.0 78.6 %copy-start.31 = (f32[256]{0:T(256)}, f32[256]{0:T(256)S(1)}, u32[]{:S(2)}) copy-start(f32[256]{0:T(256)S(1)} %broadcast_multiply_fusion.1) | copy-start | bytes 3076
  158.3 78.4 %copy-start.36 = (f32[256]{0:T(256)}, f32[256]{0:T(256)S(1)}, u32[]{:S(2)}) copy-start(f32[256]{0:T(256)S(1)} %fusion.71) | copy-start | bytes 3076
  238.3 260.4 %reduce-scatter.16.cloned.1.call-start = ((), (), s32[]{:S(2)}) async-start(), calls=%async_computation.16 | async-start | bytes 3981312
  422.3 116.8 %reduce-scatter.10.cloned.1.call-start = ((), (), s32[]{:S(2)}) async-start(), calls=%async_computation.13 | async-start | bytes 1327104 | tf_op jit(solution)/shard_map/reduce_scatter | solution.py:308
  425.1 171.3 %reduce-scatter.12.cloned.1.call-start = ((), (), s32[]{:S(2)}) async-start(), calls=%async_computation.14 | async-start | bytes 5308416 | tf_op jit(solution)/shard_map/reduce_scatter | solution.py:320
  430.5 222.9 %reduce-scatter.14.cloned.1.call-start = ((), (), s32[]{:S(2)}) async-start(), calls=%async_computation.15 | async-start | bytes 5308416 | tf_op jit(solution)/shard_map/reduce_scatter | solution.py:326
  436.7 245.6 %copy-start.1 = (f32[256,768]{1,0:T(8,128)S(1)}, f32[256,768]{1,0:T(8,128)}, u32[]{:S(2)}) copy-start(f32[256,768]{1,0:T(8,128)} %copy-done) | copy-start | bytes 2359300
  436.7 245.6 %copy-start.28 = (f32[768]{0:T(1024)S(1)}, f32[768]{0:T(1024)}, u32[]{:S(2)}) copy-start(f32[768]{0:T(1024)} %copy-done.27) | copy-start | bytes 9220
  436.8 245.6 %copy-start.30 = (f32[256]{0:T(256)S(1)}, f32[256]{0:T(256)}, u32[]{:S(2)}) copy-start(f32[256]{0:T(256)} %copy-done.29) | copy-start | bytes 3076
  436.8 247.1 %copy-start.19 = (bf16[256,12,64]{0,2,1:T(8,128)(2,1)S(1)}, bf16[256,12,64]{0,2,1:T(8,128)(2,1)}, u32[]{:S(2)}) copy-start(bf16[256,12,64]{0,2,1:T(8,128)(2,1)} %copy-done.18) | copy-start | bytes 1179652
  436.8 254.0 %reduce-scatter.18.cloned.1.call-start = ((), (), s32[]{:S(2)}) async-start(), calls=%async_computation.17 | async-start | bytes 221184
  440.5 334.0 %all-reduce.19.cloned.1.call-start = ((), (), s32[]{:S(2)}) async-start(), calls=%async_computation.18 | async-start | bytes 3833856 | tf_op jit(solution)/shard_map/psum | solution.py:340
  (46 other events, 447.2 us)
Sparse Core Ops, SparseCore 0:
  9.9 36.5 all-gather.11
  50.7 32.3 all-gather.13
  85.6 32.1 all-gather.15
  119.5 23.9 all-gather.17
  145.2 38.7 all-gather.19
  185.8 38.7 all-gather.21
  226.5 32.1 all-gather.23
  260.6 32.3 all-gather.25
  422.4 76.2 reduce-scatter.15
  502.3 36.6 reduce-scatter.9
  542.5 53.7 reduce-scatter.11
  599.6 53.7 reduce-scatter.13
  657.1 33.6 reduce-scatter.17
  693.8 80.6 all-reduce.18
where the time goes:
time: 794 us; the launch traced here: 788 us
  waiting for transfers between devices  398 us (50%)
  matrix products  130 us (16%)
  blocking collectives  103 us (13%)
  local copies, waits for them, and re-layouts  79.1 us (10%)
  loops' own time  32.1 us (4%)
  other arithmetic  27.6 us (3%)
  between operations  16.9 us (2%)
    psum x1, waiting for transfers between devices, body(): lax.psum(shard_grads[0].astype(jnp.bfloat16), 'replica').astype(jnp.float32)  66.8 us
    unnamed x16, waiting for transfers between devices  63.4 us
    reduce_scatter x1, waiting for transfers between devices, body(): lax.psum_scatter(local_grads[6].astype(jnp.bfloat16), 'shard', scatter_di...  57.3 us
    reduce_scatter x1, waiting for transfers between devices, body(): lax.psum_scatter(local_grads[8].astype(jnp.bfloat16), 'shard', scatter_di...  57.1 us
    unnamed x2, blocking collectives  47.7 us
    all_gather x1, waiting for transfers between devices, body(): lax.all_gather(w_qkv, 'shard', axis=0, tiled=True)  38.5 us
    reduce_scatter x1, waiting for transfers between devices, body(): lax.psum_scatter(local_grads[2].astype(jnp.bfloat16), 'shard', scatter_di...  38.3 us
    all_gather x1, waiting for transfers between devices, body(): lax.all_gather(w_back, 'shard', axis=0, tiled=True)  28.4 us
  transfers between devices with their start and end apart: 14, of which 11 were waited for; matrix products, arithmetic and copies ran while one was open for 19% of the time, Pallas kernels for 0%

commit v1 on v0

--- a/solution.py
+++ b/solution.py
@@ -1,13 +1,24 @@
+import functools
 import math
 import jax
 import jax.numpy as jnp
 from jax import lax
 from jax.sharding import PartitionSpec as P
+from jax.lax import all_gather
 
 HEADS = 12
 scale_factor = 0.125
 norm_epsilon = 1e-05
 masked_value = -1e30
+
+
+def corner_handle(a0, axis_key):
+    reached = all_gather(a0, axis_key)
+    state_now = jnp.sum(reached, axis=0)
+    return state_now
+
+
+finish_the_ranges = functools.partial(corner_handle, axis_key="replica")
 
 
 def normalize(resid, gain, shift):
@@ -337,7 +348,7 @@
         ).astype(jnp.float32),
     )
     total_grads = (
-        lax.psum(shard_grads[0].astype(jnp.bfloat16), "replica").astype(jnp.float32),
+        finish_the_ranges(shard_grads[0].astype(jnp.bfloat16)).astype(jnp.float32),
         lax.psum(shard_grads[1].astype(jnp.bfloat16), "replica").astype(jnp.float32),
         lax.psum(shard_grads[2].astype(jnp.bfloat16), "replica").astype(jnp.float32),
         lax.psum(shard_grads[3].astype(jnp.bfloat16), "replica").astype(jnp.float32),

time: 794 us -> 658 us (0.83)
  waiting for transfers between devices: 398 us -> 261 us
    unnamed x16, waiting for transfers between devices: 63.4 us -> 4.89 us
    reduce_scatter x1, waiting for transfers between devices: 57.3 us -> 0.02 us  [body(): lax.psum_scatter(local_grads[6].astype(jnp.bfloat16), 'shard', scatter_di...]
    reduce_scatter x0 -> x1, waiting for transfers between devices: none -> 53.5 us  [body(): lax.psum_scatter(local_grads[0].astype(jnp.bfloat16), 'shard', scatter_di...]
    reduce_scatter x1, waiting for transfers between devices: 38.3 us -> 0.02 us  [body(): lax.psum_scatter(local_grads[2].astype(jnp.bfloat16), 'shard', scatter_di...]
    reduce_scatter x1, waiting for transfers between devices: 57.1 us -> 20.1 us  [body(): lax.psum_scatter(local_grads[8].astype(jnp.bfloat16), 'shard', scatter_di...]
    all_gather x0 -> x1, waiting for transfers between devices: none -> 35 us  [corner_handle(): reached = all_gather(a0, axis_key)]
    psum x1, waiting for transfers between devices: 66.8 us -> 46.8 us  [body(): lax.psum(shard_grads[2].astype(jnp.bfloat16), 'replica').astype(jnp.float32)]
    all_gather x1, waiting for transfers between devices: 16.2 us -> 4.09 us  [body(): query_piece = lax.all_gather(query, 'shard', axis=0, tiled=True)]
  transfers between devices with their start and end apart: 14 -> 15, of which waited for: 11 -> 10; matrix products, arithmetic and copies ran while one was open for 19% -> 35% of each run, Pallas kernels for 0% -> 0%
where the time goes in v1:
time: 658 us; the launch traced here: 652 us
  waiting for transfers between devices  261 us (40%)
  matrix products  132 us (20%)
  blocking collectives  105 us (16%)
  local copies, waits for them, and re-layouts  72.2 us (11%)
  other arithmetic  32.2 us (5%)
  loops' own time  31.6 us (5%)
  between operations  16.9 us (3%)
    reduce_scatter x1, waiting for transfers between devices, body(): lax.psum_scatter(local_grads[0].astype(jnp.bfloat16), 'shard', scatter_di...  53.5 us
    unnamed x2, blocking collectives  48.1 us
    psum x1, waiting for transfers between devices, body(): lax.psum(shard_grads[2].astype(jnp.bfloat16), 'replica').astype(jnp.float32)  46.8 us
    all_gather x1, waiting for transfers between devices, body(): lax.all_gather(w_qkv, 'shard', axis=0, tiled=True)  38.5 us
    all_gather x1, waiting for transfers between devices, corner_handle(): reached = all_gather(a0, axis_key)  35 us
    all_gather x1, waiting for transfers between devices, body(): lax.all_gather(w_back, 'shard', axis=0, tiled=True)  28.7 us
    dot_general x9, matrix products, masked_scores(): jnp.einsum('qhd,khd->hqk', query_heads, key_heads, preferred_element_type...  25.7 us
    all_gather x1, waiting for transfers between devices, body(): lax.all_gather(w_in, 'shard', axis=0, tiled=True)  25.6 us
  transfers between devices with their start and end apart: 15, of which 10 were waited for; matrix products, arithmetic and copies ran while one was open for 35% of the time, Pallas kernels for 0%

profile of v1, /device:TPU:0, one launch (start us, length us, event | category | flops | bytes accessed | tf_op | source)
XLA Modules:
  0.0 652.4 jit_solution(9521956484370203380)
XLA Ops:
  8.0 38.5 %all-gather.14.cloned.1.call-done = bf16[768,2304]{1,0:T(8,128)(2,1)} async-done(((bf16[96,2304]{1,0:T(8,128)(2,1)}), bf16[768,2304]{1,0:T(8,128)(2,1)}) %all-gather.14.cloned.1.call-update) | async-done | bytes 3538960 | tf_op jit(solution)/shard_map/all_gather | solution.py:85
  50.7 8.7 %all-gather.2 = bf16[8,96,2]{1,2,0:T(2,128)(2,1)S(1)} all-gather(bf16[1,96,2]{1,2,0:T(2,128)(2,1)S(1)} %bitcast.174), channel_id=1, replica_groups=mesh['shard'=8,'replica'=4] {'shard'}, dimensions={0}, use_global_device_ids=true | all-gather | bytes 3456 | tf_op jit(solution)/shard_map/all_gather | solution.py:87
  64.6 24.2 %all-reduce.14 = (bf16[768]{0:T(1024)(128)(2,1)S(1)}, bf16[768]{0:T(1024)(128)(2,1)S(1)}, bf16[768]{0:T(1024)(128)(2,1)S(1)}, bf16[768]{0:T(1024)(128)(2,1)S(1)}, bf16[768]{0:T(1024)(128)(2,1)S(1)}) all-reduce(bf16[768]{0:T(1024)(128)(2,1)S(1)} %dynamic-update-slice, ...), channel_id=1, replica_groups=mesh['shard'=8,'replica'=4] {'shard'}, use_global_device_ids=true, to_apply=%add | all-reduce | flops 3840 | bytes 15360
  97.0 9.8 %all-gather.1 = s32[8,1,256]{2,1,0:T(1,128)} all-gather(s32[1,1,256]{2,1,0:T(1,128)S(1)} %bitcast.170), channel_id=1, replica_groups=mesh['shard'=8,'replica'=4] {'shard'}, dimensions={0}, use_global_device_ids=true | all-gather | bytes 9216 | tf_op jit(solution)/shard_map/all_gather | solution.py:107
  122.0 32.9 %while.48 = (s32[]{:T(128)}, f32[12,256]{1,0:T(8,128)S(1)}, f32[12,256]{1,0:T(8,128)S(1)}, f32[256,12,64]{0,2,1:T(8,128)S(1)}, s32[2048]{0:T(1024)}, /*index=5*/...) while((s32[]{:T(128)}, f32[12,256]{1,0:T(8,128)S(1)}, ...), condition=%wide.region_5.6_spmd, body=%wide.region_0.5_spmd.sunk | while | flops 420488192 | bytes 26287476 | solution.py:141
  157.9 25.6 %all-gather.22.cloned.1.call-done = bf16[768,3072]{1,0:T(8,128)(2,1)} async-done(((bf16[96,3072]{1,0:T(8,128)(2,1)}), bf16[768,3072]{1,0:T(8,128)(2,1)}) %all-gather.22.cloned.1.call-update) | async-done | bytes 4718608 | tf_op jit(solution)/shard_map/all_gather | solution.py:154
  183.5 11.8 %multiply_convert_fusion.8 = (bf16[256,3072]{1,0:T(8,128)(2,1)}, f32[256,3072]{1,0:T(8,128)}, f32[256,3072]{1,0:T(8,128)}) fusion(f32[3072]{0:T(1024)S(1)} %bitcast.173, bf16[768,3072]{1,0:T(8,128)(2,1)} %all-gather.22.cloned.1.call-done, f32[256,768]{1,0:T(8,128)S(1)} %get-tuple-element.1189, f32[768]{0:T(1024)S(1)} %convert_element_type.211, ...), kind=kOutput, calls=%fused_computation.63 | convolution fusion | flops 1260847104 | bytes 13389824 | tf_op jit(solution)/shard_map/dot_general | solution.py:162
  195.3 28.7 %all-gather.24.cloned.1.call-done = bf16[3072,768]{1,0:T(8,128)(2,1)} async-done(((bf16[384,768]{1,0:T(8,128)(2,1)}), bf16[3072,768]{1,0:T(8,128)(2,1)}) %all-gather.24.cloned.1.call-update) | async-done | bytes 4718608 | tf_op jit(solution)/shard_map/all_gather | solution.py:156
  263.5 9.3 %all_gather.83 = f32[12,2048]{1,0:T(8,128)S(1)} all-gather(f32[12,256]{1,0:T(8,128)} %log_add_fusion), channel_id=1, replica_groups=mesh['shard'=8,'replica'=4] {'shard'}, dimensions={1}, use_global_device_ids=true | all-gather | bytes 110592 | tf_op jit(solution)/shard_map/all_gather | solution.py:238
  274.5 8.8 %all_gather.85 = f32[12,2048]{1,0:T(8,128)S(1)} all-gather(f32[12,256]{1,0:T(8,128)} %fusion.66), channel_id=1, replica_groups=mesh['shard'=8,'replica'=4] {'shard'}, dimensions={1}, use_global_device_ids=true | all-gather | bytes 110592 | tf_op jit(solution)/shard_map/all_gather | solution.py:239
  284.2 51.4 %while.49 = (s32[]{:T(128)}, f32[256,12,64]{0,2,1:T(8,128)}, s32[2048]{0:T(1024)}, s32[]{:T(128)}, s32[]{:T(128)}, /*index=5*/s32[256]{0:T(256)}, bf16[2048,768]...) while((s32[]{:T(128)}, f32[256,12,64]{0,2,1:T(8,128)}, ...), condition=%wide.region_17.18_spmd, body=%wide.region_14.17_spmd.sunk | while | flops 613941248 | bytes 20745584 | solution.py:236
  288.1 11.9 %conditional.7 = (f32[256,12,64]{0,2,1:T(8,128)}) conditional(s32[]{:T(128)} %convert_element_type.317, f32[256,12,64]{0,2,1:T(8,128)} %get-tuple-element.1513, (s32[256]{0:T(256)}, s32[512]{0:T(512)S(1)}, bf16[2048,768]{0,1:T(8,128)(2,1)}, s32[]{:T(128)}, bf16[256,12,64]{0,2,1:T(8,128)(2,1)S(1)}, /*index=5*/f32[12,256]{1,0:T(8,128)}, ...), branch_computations={%region_15.15_spmd, %region_16.16_spmd} | conditional | flops 613941248 | bytes 20741160 | solution.py:234
  304.0 11.9 %conditional.7 = (f32[256,12,64]{0,2,1:T(8,128)}) conditional(s32[]{:T(128)} %convert_element_type.317, f32[256,12,64]{0,2,1:T(8,128)} %get-tuple-element.1513, (s32[256]{0:T(256)}, s32[512]{0:T(512)S(1)}, bf16[2048,768]{0,1:T(8,128)(2,1)}, s32[]{:T(128)}, bf16[256,12,64]{0,2,1:T(8,128)(2,1)S(1)}, /*index=5*/f32[12,256]{1,0:T(8,128)}, ...), branch_computations={%region_15.15_spmd, %region_16.16_spmd} | conditional | flops 613941248 | bytes 20741160 | solution.py:234
  319.8 11.9 %conditional.7 = (f32[256,12,64]{0,2,1:T(8,128)}) conditional(s32[]{:T(128)} %convert_element_type.317, f32[256,12,64]{0,2,1:T(8,128)} %get-tuple-element.1513, (s32[256]{0:T(256)}, s32[512]{0:T(512)S(1)}, bf16[2048,768]{0,1:T(8,128)(2,1)}, s32[]{:T(128)}, bf16[256,12,64]{0,2,1:T(8,128)(2,1)S(1)}, /*index=5*/f32[12,256]{1,0:T(8,128)}, ...), branch_computations={%region_15.15_spmd, %region_16.16_spmd} | conditional | flops 613941248 | bytes 20741160 | solution.py:234
  342.4 68.2 %while.50 = (s32[]{:T(128)}, f32[256,12,64]{0,2,1:T(8,128)}, f32[256,12,64]{0,2,1:T(8,128)}, s32[2048]{0:T(1024)}, s32[]{:T(128)}, /*index=5*/s32[]{:T(128)}, s3...) while((s32[]{:T(128)}, f32[256,12,64]{0,2,1:T(8,128)}, ...), condition=%wide.region_21.22_spmd, body=%wide.region_18.21_spmd.sunk | while | flops 821755904 | bytes 29670792 | solution.py:286
  346.3 17.4 %conditional.8 = ((f32[256,12,64]{0,2,1:T(8,128)}, f32[256,12,64]{0,2,1:T(8,128)})) conditional(s32[]{:T(128)} %convert_element_type.318, (f32[256,12,64]{0,2,1:T(8,128)}, f32[256,12,64]{0,2,1:T(8,128)}) %tuple.170, (s32[512]{0:T(512)S(1)}, s32[256]{0:T(256)S(1)}, bf16[2048,768]{0,1:T(8,128)(2,1)}, s32[]{:T(128)}, ...), branch_computations={%region_19.19_spmd, %region_20.20_spmd} | conditional | flops 821755904 | bytes 29666336 | solution.py:284
  367.7 17.2 %conditional.8 = ((f32[256,12,64]{0,2,1:T(8,128)}, f32[256,12,64]{0,2,1:T(8,128)})) conditional(s32[]{:T(128)} %convert_element_type.318, (f32[256,12,64]{0,2,1:T(8,128)}, f32[256,12,64]{0,2,1:T(8,128)}) %tuple.170, (s32[512]{0:T(512)S(1)}, s32[256]{0:T(256)S(1)}, bf16[2048,768]{0,1:T(8,128)(2,1)}, s32[]{:T(128)}, ...), branch_computations={%region_19.19_spmd, %region_20.20_spmd} | conditional | flops 821755904 | bytes 29666336 | solution.py:284
  388.8 17.7 %conditional.8 = ((f32[256,12,64]{0,2,1:T(8,128)}, f32[256,12,64]{0,2,1:T(8,128)})) conditional(s32[]{:T(128)} %convert_element_type.318, (f32[256,12,64]{0,2,1:T(8,128)}, f32[256,12,64]{0,2,1:T(8,128)}) %tuple.170, (s32[512]{0:T(512)S(1)}, s32[256]{0:T(256)S(1)}, bf16[2048,768]{0,1:T(8,128)(2,1)}, s32[]{:T(128)}, ...), branch_computations={%region_19.19_spmd, %region_20.20_spmd} | conditional | flops 821755904 | bytes 29666336 | solution.py:284
  427.2 20.1 %reduce-scatter.14.cloned.1.call-done = bf16[384,768]{1,0:T(8,128)(2,1)} async-done(((bf16[3072,768]{1,0:T(8,128)(2,1)}), bf16[384,768]{1,0:T(8,128)(2,1)}) %reduce-scatter.14.cloned.1.call-update) | async-done | bytes 589840 | tf_op jit(solution)/shard_map/reduce_scatter | solution.py:337
  447.4 53.5 %reduce-scatter.16.cloned.1.call-done = bf16[96,2304]{1,0:T(8,128)(2,1)} async-done(((bf16[768,2304]{1,0:T(8,128)(2,1)}), bf16[96,2304]{1,0:T(8,128)(2,1)}) %reduce-scatter.16.cloned.1.call-update) | async-done | bytes 442384 | tf_op jit(solution)/shard_map/reduce_scatter | solution.py:313
  505.7 23.9 %all-reduce.13 = (bf16[768]{0:T(1024)(128)(2,1)S(1)}, bf16[768]{0:T(1024)(128)(2,1)S(1)}, bf16[768]{0:T(1024)(128)(2,1)S(1)}, bf16[768]{0:T(1024)(128)(2,1)S(1)}...) all-reduce(bf16[768]{0:T(1024)(128)(2,1)} %dynamic-update-slice.5, ...), channel_id=1, replica_groups=mesh['shard'=8,'replica'=4] {'shard'}, use_global_device_ids=true, to_apply=%add.5 | all-reduce | flops 8448 | bytes 33792
  539.0 11.9 %all-reduce.15 = (bf16[2,96]{1,0:T(2,128)(2,1)S(1)}, bf16[96]{0:T(256)(128)(2,1)S(1)}, bf16[96]{0:T(256)(128)(2,1)S(1)}, bf16[96]{0:T(256)(128)(2,1)S(1)}, bf16[...) all-reduce(bf16[2,96]{1,0:T(2,128)(2,1)S(1)} %copy.94, ...), channel_id=1, replica_groups=mesh['shard'=8,'replica'=4] {'replica'}, use_global_device_ids=true, to_apply=%region_27.28 | all-reduce | flops 1152 | bytes 4608 | tf_op jit(solution)/shard_map/psum | solution.py:352
  555.1 46.8 %all-reduce.19.cloned.1.call-done = (bf16[96,768]{1,0:T(8,128)(2,1)}, bf16[96,3072]{1,0:T(8,128)(2,1)}, bf16[384,768]{1,0:T(8,128)(2,1)}) async-done(((bf16[96,768]{1,0:T(8,128)(2,1)}, bf16[96,3072]{1,0:T(8,128)(2,1)}, bf16[384,768]{1,0:T(8,128)(2,1)}), (bf16[96,768]{1,0:T(8,128)(2,1)}, bf16[96,3072]{1,0:T(8,128)(2,1)}, bf16[384,768]{1,0:T(8,128)(2,1)})) %all-reduce.19.cloned.1.call-update) | async-done | bytes 1327120 | tf_op jit(solution)/shard_map/psum | solution.py:353
  607.9 35.0 %all-gather.30.cloned.1.call-done = bf16[384,2304]{1,0:T(8,128)(2,1)} async-done(((bf16[96,2304]{1,0:T(8,128)(2,1)}), bf16[384,2304]{1,0:T(8,128)(2,1)}) %all-gather.30.cloned.1.call-update) | async-done | bytes 1769488 | tf_op jit(solution)/shard_map/all_gather | solution.py:16
  (322 shorter events, 264.3 us)
Async XLA Ops:
  7.2 39.3 %all-gather.14.cloned.1.call-start = ((), (), s32[]{:S(2)}) async-start(), calls=%async_computation.5 | async-start | bytes 3981312 | tf_op jit(solution)/shard_map/all_gather | solution.py:85
  7.9 100.3 %all-gather.16.cloned.1.call-start = ((), (), s32[]{:S(2)}) async-start(), calls=%async_computation.6 | async-start | bytes 3538944 | tf_op jit(solution)/shard_map/all_gather | solution.py:105
  49.8 47.2 %copy-start.18 = (s32[256]{0:T(256)S(1)}, s32[256]{0:T(256)}, u32[]{:S(2)}) copy-start(s32[256]{0:T(256)} %param.28) | copy-start | bytes 3076
  50.6 66.6 %all-gather.18.cloned.1.call-start = ((), (), s32[]{:S(2)}) async-start(), calls=%async_computation.7 | async-start | bytes 3538944 | tf_op jit(solution)/shard_map/all_gather | solution.py:106
  60.4 94.6 %all-gather.20.cloned.1.call-start = ((), (), s32[]{:S(2)}) async-start(), calls=%async_computation.8 | async-start | bytes 1327104 | tf_op jit(solution)/shard_map/all_gather | solution.py:86
  61.0 122.5 %all-gather.22.cloned.1.call-start = ((), (), s32[]{:S(2)}) async-start(), calls=%async_computation.9 | async-start | bytes 5308416 | tf_op jit(solution)/shard_map/all_gather | solution.py:154
  61.6 162.5 %all-gather.24.cloned.1.call-start = ((), (), s32[]{:S(2)}) async-start(), calls=%async_computation.10 | async-start | bytes 5308416 | tf_op jit(solution)/shard_map/all_gather | solution.py:156
  62.1 196.0 %all-gather.26.cloned.1.call-start = ((), (), s32[]{:S(2)}) async-start(), calls=%async_computation.11 | async-start | bytes 3538944 | tf_op jit(solution)/shard_map/all_gather | solution.py:241
  96.9 127.1 %copy-start.23 = (f32[768]{0:T(1024)}, f32[768]{0:T(1024)S(1)}, u32[]{:S(2)}) copy-start(f32[768]{0:T(1024)S(1)} %convert_element_type.211) | copy-start | bytes 9220
  97.0 127.1 %copy-start.21 = (f32[768]{0:T(1024)}, f32[768]{0:T(1024)S(1)}, u32[]{:S(2)}) copy-start(f32[768]{0:T(1024)S(1)} %convert_element_type.210) | copy-start | bytes 9220
  97.0 131.8 %copy-start.25 = (f32[768]{0:T(1024)}, f32[768]{0:T(1024)S(1)}, u32[]{:S(2)}) copy-start(f32[768]{0:T(1024)S(1)} %convert_element_type.216) | copy-start | bytes 9220
  107.6 228.1 %all-gather.28.cloned.1.call-start = ((), (), s32[]{:S(2)}) async-start(), calls=%async_computation.12 | async-start | bytes 3538944 | tf_op jit(solution)/shard_map/all_gather | solution.py:242
  237.9 189.4 %reduce-scatter.10.cloned.1.call-start = ((), (), s32[]{:S(2)}) async-start(), calls=%async_computation.13 | async-start | bytes 1327104 | tf_op jit(solution)/shard_map/reduce_scatter | solution.py:319
  239.5 187.7 %reduce-scatter.12.cloned.1.call-start = ((), (), s32[]{:S(2)}) async-start(), calls=%async_computation.14 | async-start | bytes 5308416 | tf_op jit(solution)/shard_map/reduce_scatter | solution.py:331
  244.8 202.6 %reduce-scatter.14.cloned.1.call-start = ((), (), s32[]{:S(2)}) async-start(), calls=%async_computation.15 | async-start | bytes 5308416 | tf_op jit(solution)/shard_map/reduce_scatter | solution.py:337
  251.0 249.8 %reduce-scatter.16.cloned.1.call-start = ((), (), s32[]{:S(2)}) async-start(), calls=%async_computation.17 | async-start | bytes 3981312 | tf_op jit(solution)/shard_map/reduce_scatter | solution.py:313
  423.3 80.8 %copy-start.1 = (f32[256,768]{1,0:T(8,128)S(1)}, f32[256,768]{1,0:T(8,128)}, u32[]{:S(2)}) copy-start(f32[256,768]{1,0:T(8,128)} %copy-done) | copy-start | bytes 2359300
  423.3 80.8 %copy-start.30 = (f32[256]{0:T(256)S(1)}, f32[256]{0:T(256)}, u32[]{:S(2)}) copy-start(f32[256]{0:T(256)} %copy-done.29) | copy-start | bytes 3076
  423.3 80.9 %copy-start.6 = (f32[256,768]{1,0:T(8,128)S(1)}, f32[256,768]{1,0:T(8,128)}, u32[]{:S(2)}) copy-start(f32[256,768]{1,0:T(8,128)} %copy-done.4) | copy-start | bytes 2359300
  423.4 106.8 %copy-start.26 = (f32[768]{0:T(1024)S(1)}, f32[768]{0:T(1024)}, u32[]{:S(2)}) copy-start(f32[768]{0:T(1024)} %copy-done.25) | copy-start | bytes 9220
  423.4 106.8 %copy-start.28 = (f32[256]{0:T(256)S(1)}, f32[256]{0:T(256)}, u32[]{:S(2)}) copy-start(f32[256]{0:T(256)} %copy-done.27) | copy-start | bytes 3076
  423.4 114.8 %reduce-scatter.18.cloned.1.call-start = ((), (), s32[]{:S(2)}) async-start(), calls=%async_computation.18 | async-start | bytes 221184
  427.1 174.8 %all-reduce.19.cloned.1.call-start = ((), (), s32[]{:S(2)}) async-start(), calls=%async_computation.19 | async-start | bytes 2654208 | tf_op jit(solution)/shard_map/psum | solution.py:353
  447.3 195.5 %all-gather.30.cloned.1.call-start = ((), (), s32[]{:S(2)}) async-start(), calls=%async_computation.16 | async-start | bytes 2211840 | tf_op jit(solution)/shard_map/all_gather | solution.py:16
  (40 other events, 418.7 us)
Sparse Core Ops, SparseCore 0:
  9.9 36.5 all-gather.13
  50.7 32.3 all-gather.15
  85.0 32.1 all-gather.17
  118.9 23.9 all-gather.19
  144.6 38.7 all-gather.21
  185.2 38.7 all-gather.23
  225.9 32.1 all-gather.25
  260.0 32.3 all-gather.27
  296.2 36.6 reduce-scatter.9
  336.2 53.7 reduce-scatter.11
  393.5 53.7 reduce-scatter.13
  450.7 50.1 reduce-scatter.15
  504.5 33.6 reduce-scatter.17
  540.6 61.2 all-reduce.18
  603.3 39.4 all-gather.29
